TPU v7x, 32 devices: a whole 2x2x4 slice. The times are simulated.
32 devices in a mesh: dp: 4 (over y, core), mp: 8 (over z, x).
Axes of the slice: x: 2, y: 2, z: 4, core: 2. Of those that a mesh axis runs over, the one named last changes fastest.
Arguments:
- block_in: bfloat16 [8192, 768], P(('dp', 'mp')), may hold values from -6 to 6
- segment_ids: int32 [8192], P('dp'), may hold values from 0 to 8191, as said below
- w_qkv: bfloat16 [768, 2304], P(('dp', 'mp')), may hold values from -0.21875 to 0.21875
- w_out: bfloat16 [768, 768], P(('dp', 'mp')), may hold values from -0.875 to 0.875
- conv_taps: bfloat16 [768, 3, 3], P(('dp', 'mp')), may hold values from -4 to 4
- norm_gain: bfloat16 [768, 2], P(('dp', 'mp')), may hold values from 0.5 to 1.5
- norm_bias: bfloat16 [768, 2], P(('dp', 'mp')), may hold values from -3 to 3
- w_up: bfloat16 [768, 3072], P(None, 'mp'), may hold values from -0.21875 to 0.21875
- w_down: bfloat16 [3072, 768], P('mp'), may hold values from -0.109375 to 0.109375
- out_grad: bfloat16 [8192, 768], P(('dp', 'mp')), may hold values from -6 to 6
Outputs:
- block_out: bfloat16 [8192, 768], P(('dp', 'mp'))
- input_grad: float32 [8192, 768], P(('dp', 'mp'))
- qkv_grad: float32 [768, 2304], P(('dp', 'mp'))
- proj_grad: float32 [768, 768], P(('dp', 'mp'))
- conv_grad: float32 [768, 3, 3], P(('dp', 'mp'))
- gain_grad: float32 [768, 2], P(('dp', 'mp'))
- bias_grad: float32 [768, 2], P(('dp', 'mp'))
- up_grad: float32 [768, 3072], P(None, 'mp')
- down_grad: float32 [3072, 768], P('mp')
Inputs may be any that keep to these rules, and one draw needn't show every extreme that they name: `segment_ids`: segment ids never fall along the tokens, and tokens with equal ids form one document. A token's id is its packed sequence times 2048 plus the place, within that sequence, of its document's last token. The first token of each packed sequence is a document of its own; each document holds at most 1024 tokens, and every packed sequence has one of exactly that many.
All inputs are finite; a program needn't handle non-finite values.
Results may differ from a plain program's by a relative error of at most 0.018.
The roundings to bfloat16 on the way count: a program that leaves them out, or rounds other values in their place, can miss the bound.
Values may be sent and summed in bfloat16 or wider, within the bound.
A program may use at most 128 MiB of HBM per device.

v0:
```python
import jax
import jax.numpy as jnp
from jax import lax
from jax.sharding import PartitionSpec as P

HEAD_DIM = 64
eps_norm = 1e-05


def from_behind(value, axis, steps):
    count = lax.axis_size(axis)
    leading, last = (max(0, -steps), min(count, count - steps))
    return lax.ppermute(value, axis, [(source, source + steps) for source in range(leading, last)])


def layer_norm(rows, gain, bias):
    average = jnp.mean(rows, axis=-1, keepdims=True)
    centered = rows - average
    spread = jnp.mean(centered * centered, axis=-1, keepdims=True)
    inverse = lax.rsqrt(spread + eps_norm)
    normal = centered * inverse
    return (normal * gain + bias, normal, inverse)


def norm_back(grad, normal, inverse, gain):
    scaled = grad * gain
    inner = (
        scaled
        - jnp.mean(scaled, axis=-1, keepdims=True)
        - normal * jnp.mean(scaled * normal, axis=-1, keepdims=True)
    )
    return (inner * inverse, jnp.sum(grad * normal, axis=0), jnp.sum(grad, axis=0))


def tap_keep(segs, places, here, there, count, seq_len):
    same_segment = segs[here : here + count] == segs[there : there + count]
    same_sequence = (
        places[here : here + count] // seq_len == places[there : there + count] // seq_len
    )
    return (same_segment & same_sequence)[:, None]


def conv_apply(pre_wide, taps, segs, places, seq_len):
    count = pre_wide.shape[0] - 2
    total = jnp.zeros((count, pre_wide.shape[1]), jnp.float32)
    for lag in range(3):
        keep = tap_keep(segs, places, 2, 2 - lag, count, seq_len)
        total = total + jnp.where(keep, pre_wide[2 - lag : 2 - lag + count], 0.0) * taps[lag]
    return total


def conv_back(grad_wide, taps, segs, places, seq_len):
    count = grad_wide.shape[0] - 2
    total = jnp.zeros((count, grad_wide.shape[1]), jnp.float32)
    for lag in range(3):
        keep = tap_keep(segs, places, lag, 0, count, seq_len)
        total = total + jnp.where(keep, grad_wide[lag : lag + count], 0.0) * taps[lag]
    return total


def taps_back(pre_wide, grad, segs, places, seq_len):
    count = grad.shape[0]
    results = []
    for lag in range(3):
        keep = tap_keep(segs, places, 2, 2 - lag, count, seq_len)
        results.append(
            jnp.sum(jnp.where(keep, pre_wide[2 - lag : 2 - lag + count] * grad, 0.0), axis=0)
        )
    return jnp.stack(results)


def contract_first(left, right):
    return lax.dot_general(
        left, right, (((0,), (0,)), ((), ())), preferred_element_type=jnp.float32
    )


def contract_last(left, right):
    return lax.dot_general(
        left, right, (((1,), (1,)), ((), ())), preferred_element_type=jnp.float32
    )


def on_device(
    block_in, segment_ids, w_qkv, w_out, conv_taps, norm_gain, norm_bias, w_up, w_down, out_grad
):
    rows, width = block_in.shape
    heads = width // HEAD_DIM
    block = min(512, rows)
    reach = lax.axis_size("mp")
    seq_len = rows * reach
    scale = HEAD_DIM ** (-0.5)
    model_index = lax.axis_index("mp")
    start = model_index * rows
    offset = (reach - 1 - model_index) * rows
    seq_begin = start - model_index * rows
    full_qkv, full_out, full_taps, full_gain, full_bias = (
        lax.all_gather(w_qkv, ("dp", "mp"), axis=0, tiled=True),
        lax.all_gather(w_out, ("dp", "mp"), axis=0, tiled=True),
        lax.all_gather(conv_taps, ("dp", "mp"), axis=0, tiled=True),
        lax.all_gather(norm_gain, ("dp", "mp"), axis=0, tiled=True),
        lax.all_gather(norm_bias, ("dp", "mp"), axis=0, tiled=True),
    )
    gains = full_gain.astype(jnp.float32)
    biases = full_bias.astype(jnp.float32)
    taps = full_taps.astype(jnp.float32).transpose(1, 0, 2).reshape(3 * width, 3).T
    padding = jnp.full((2,), -1, jnp.int32)
    padded_segs = jnp.concatenate([padding, segment_ids, padding])
    back_segs = lax.dynamic_slice_in_dim(padded_segs, start, rows + 2)
    back_places = start - 2 + jnp.arange(rows + 2, dtype=jnp.int32)
    ahead_segs = lax.dynamic_slice_in_dim(padded_segs, start + 2, rows + 2)
    ahead_places = start + jnp.arange(rows + 2, dtype=jnp.int32)
    inputs = block_in.astype(jnp.float32)
    normed1_full, normal1, inverse1 = layer_norm(inputs, gains[:, 0], biases[:, 0])
    normed1 = normed1_full.astype(jnp.bfloat16)
    pre_own = jnp.dot(normed1, full_qkv, preferred_element_type=jnp.float32)
    rim = from_behind(pre_own[rows - 2 :], "mp", 1)
    pre_wide = jnp.concatenate([rim, pre_own], axis=0)
    mixed_qkv = conv_apply(pre_wide, taps, back_segs, back_places, seq_len).astype(jnp.bfloat16)
    query_rows = mixed_qkv[:, :width]
    pair_own = mixed_qkv[:, width:]
    window_start = jnp.zeros((reach * rows, 2 * width), jnp.bfloat16)
    window_start = lax.dynamic_update_slice_in_dim(window_start, pair_own, (reach - 1) * rows, 0)

    def pass_step(distance, carry):
        piece, gathered = carry
        piece = from_behind(piece, "mp", 1)
        gathered = lax.dynamic_update_slice_in_dim(
            gathered, piece, (reach - 1 - distance) * rows, 0
        )
        return (piece, gathered)

    unused_piece, window = lax.fori_loop(1, reach, pass_step, (pair_own, window_start))

    def fetch(queries, query_places, query_segs, index):
        pair = lax.dynamic_slice_in_dim(window, offset + index * block, block, 0)
        keys = pair[:, :width].reshape(block, heads, HEAD_DIM)
        values = pair[:, width:].reshape(block, heads, HEAD_DIM)
        key_places = seq_begin + index * block + jnp.arange(block, dtype=jnp.int32)
        key_segs = lax.dynamic_slice_in_dim(segment_ids, seq_begin + index * block, block)
        allowed = (
            (key_places[None, :] <= query_places[:, None])
            & (key_segs[None, :] == query_segs[:, None])
        )[None]
        scores = (
            jnp.einsum("qhd,khd->hqk", queries, keys, preferred_element_type=jnp.float32) * scale
        )
        return (keys, values, allowed, jnp.where(allowed, scores, -1e30))

    def block_setup(number):
        query_places = start + number * block + jnp.arange(block, dtype=jnp.int32)
        query_segs = lax.dynamic_slice_in_dim(segment_ids, start + number * block, block)
        queries = query_rows.reshape(block, heads, HEAD_DIM)
        count = (model_index * rows + number * block) // block + 1
        return (query_places, query_segs, queries, count)

    number = 0
    query_places, query_segs, queries, count = block_setup(number)

    def stats_step(index, carry):
        highest, total = carry
        keys, values, allowed, scores = fetch(queries, query_places, query_segs, index)
        new_high = jnp.maximum(highest, jnp.max(scores, axis=-1))
        total = total * jnp.exp(highest - new_high) + jnp.sum(
            jnp.where(allowed, jnp.exp(scores - new_high[..., None]), 0.0), axis=-1
        )
        return (new_high, total)

    highest, total = lax.fori_loop(
        0,
        count,
        stats_step,
        (jnp.full((heads, block), -1e30, jnp.float32), jnp.zeros((heads, block), jnp.float32)),
    )
    log_total = highest + jnp.log(total)

    def value_step(index, weighted):
        keys, values, allowed, scores = fetch(queries, query_places, query_segs, index)
        probs = jnp.where(allowed, jnp.exp(scores - log_total[..., None]), 0.0).astype(jnp.bfloat16)
        return weighted + jnp.einsum(
            "hqk,khd->qhd", probs, values, preferred_element_type=jnp.float32
        )

    weighted = lax.fori_loop(0, count, value_step, jnp.zeros((block, heads, HEAD_DIM), jnp.float32))
    attended_parts = weighted.reshape(block, width)
    log_parts = [log_total]
    attended = attended_parts.astype(jnp.bfloat16)
    mixed = jnp.dot(attended, full_out, preferred_element_type=jnp.float32)
    residual = inputs + mixed
    normed2_full, normal2, inverse2 = layer_norm(residual, gains[:, 1], biases[:, 1])
    normed2 = normed2_full.astype(jnp.bfloat16)
    normed2_rows = lax.all_gather(normed2, "mp", axis=0, tiled=True)
    upper = jnp.dot(normed2_rows, w_up, preferred_element_type=jnp.float32)
    hidden = jnp.square(jnp.maximum(upper, 0.0)).astype(jnp.bfloat16)
    ff_out = lax.psum_scatter(
        jnp.dot(hidden, w_down, preferred_element_type=jnp.float32).astype(jnp.bfloat16),
        "mp",
        scatter_dimension=0,
        tiled=True,
    ).astype(jnp.float32)
    block_out = (residual + ff_out).astype(jnp.bfloat16)
    grad_all = lax.all_gather(out_grad, "mp", axis=0, tiled=True)
    hidden_grad = contract_last(grad_all, w_down)
    upper_grad = (2.0 * jnp.maximum(upper, 0.0) * hidden_grad).astype(jnp.bfloat16)
    down_local = contract_first(hidden, grad_all)
    up_local = contract_first(normed2_rows, upper_grad)
    normed2_grad = lax.psum_scatter(
        contract_last(upper_grad, w_up).astype(jnp.bfloat16), "mp", scatter_dimension=0, tiled=True
    ).astype(jnp.float32)
    up_grad, down_grad = (
        lax.psum(up_local.astype(jnp.bfloat16), "dp").astype(jnp.float32),
        lax.psum(down_local.astype(jnp.bfloat16), "dp").astype(jnp.float32),
    )
    back2, gain2_grad, bias2_grad = norm_back(normed2_grad, normal2, inverse2, gains[:, 1])
    residual_grad = out_grad.astype(jnp.float32) + back2
    mixed_grad = residual_grad.astype(jnp.bfloat16)
    proj_local = contract_first(attended, mixed_grad)
    attended_grad = contract_last(mixed_grad, full_out).astype(jnp.bfloat16)
    window_grad = jnp.zeros((window.shape[0], 2 * width), jnp.float32)
    number = 0
    query_places, query_segs, queries, count = block_setup(number)
    log_total = log_parts[number]
    upstream = attended_grad.reshape(block, heads, HEAD_DIM)

    def delta_step(index, delta):
        keys, values, allowed, scores = fetch(queries, query_places, query_segs, index)
        probs = jnp.where(allowed, jnp.exp(scores - log_total[..., None]), 0.0)
        prob_grad = jnp.einsum("qhd,khd->hqk", upstream, values, preferred_element_type=jnp.float32)
        return delta + jnp.sum(probs * prob_grad, axis=-1)

    delta = lax.fori_loop(0, count, delta_step, jnp.zeros((heads, block), jnp.float32))

    def grad_step(index, carry):
        query_grad, window_grad = carry
        keys, values, allowed, scores = fetch(queries, query_places, query_segs, index)
        probs = jnp.where(allowed, jnp.exp(scores - log_total[..., None]), 0.0)
        prob_grad = jnp.einsum("qhd,khd->hqk", upstream, values, preferred_element_type=jnp.float32)
        score_grad = (probs * (prob_grad - delta[..., None])).astype(jnp.bfloat16)
        query_grad = (
            query_grad
            + jnp.einsum("hqk,khd->qhd", score_grad, keys, preferred_element_type=jnp.float32)
            * scale
        )
        key_grad = (
            jnp.einsum("hqk,qhd->khd", score_grad, queries, preferred_element_type=jnp.float32)
            * scale
        )
        value_grad = jnp.einsum(
            "hqk,qhd->khd", probs.astype(jnp.bfloat16), upstream, preferred_element_type=jnp.float32
        )
        update = jnp.concatenate(
            [key_grad.reshape(block, width), value_grad.reshape(block, width)], axis=1
        )
        place = offset + index * block
        current = lax.dynamic_slice_in_dim(window_grad, place, block, 0)
        window_grad = lax.dynamic_update_slice_in_dim(window_grad, current + update, place, 0)
        return (query_grad, window_grad)

    query_grad, window_grad = lax.fori_loop(
        0, count, grad_step, (jnp.zeros((block, heads, HEAD_DIM), jnp.float32), window_grad)
    )
    query_grads = query_grad.reshape(block, width)

    def window_slot(distance):
        return lax.dynamic_slice_in_dim(window_grad, (reach - 1 - distance) * rows, rows, 0)

    def back_step(step, gathered):
        distance = reach - 1 - step
        return from_behind(gathered.astype(jnp.bfloat16), "mp", -1).astype(
            gathered.dtype
        ) + window_slot(distance - 1)

    pair_grad = lax.fori_loop(0, reach - 1, back_step, window_slot(reach - 1))
    mix_grad = jnp.concatenate([query_grads, pair_grad], axis=1)
    ahead = from_behind(mix_grad[:2], "mp", -1)
    pre_grad = conv_back(
        jnp.concatenate([mix_grad, ahead], axis=0), taps, ahead_segs, ahead_places, seq_len
    ).astype(jnp.bfloat16)
    taps_local = taps_back(pre_wide, mix_grad, back_segs, back_places, seq_len)
    conv_local = taps_local.reshape(3, 3, width).transpose(2, 1, 0)
    normed1_grad = contract_last(pre_grad, full_qkv)
    qkv_local = contract_first(normed1, pre_grad)
    back1, gain1_grad, bias1_grad = norm_back(normed1_grad, normal1, inverse1, gains[:, 0])
    input_grad = residual_grad + back1
    gain_local = jnp.stack([gain1_grad, gain2_grad], axis=1)
    bias_local = jnp.stack([bias1_grad, bias2_grad], axis=1)
    qkv_grad, proj_grad, conv_grad, gain_grad, bias_grad = (
        lax.psum_scatter(qkv_local, ("dp", "mp"), scatter_dimension=0, tiled=True),
        lax.psum_scatter(proj_local, ("dp", "mp"), scatter_dimension=0, tiled=True),
        lax.psum_scatter(conv_local, ("dp", "mp"), scatter_dimension=0, tiled=True),
        lax.psum_scatter(gain_local, ("dp", "mp"), scatter_dimension=0, tiled=True),
        lax.psum_scatter(bias_local, ("dp", "mp"), scatter_dimension=0, tiled=True),
    )
    return (
        block_out,
        input_grad,
        qkv_grad,
        proj_grad,
        conv_grad,
        gain_grad,
        bias_grad,
        up_grad,
        down_grad,
    )


def solution(mesh):
    in_specs = (
        P(("dp", "mp"), None),
        P("dp"),
        P(("dp", "mp"), None),
        P(("dp", "mp"), None),
        P(("dp", "mp"), None, None),
        P(("dp", "mp"), None),
        P(("dp", "mp"), None),
        P(None, "mp"),
        P("mp", None),
        P(("dp", "mp"), None),
    )
    out_specs = (
        P(("dp", "mp"), None),
        P(("dp", "mp"), None),
        P(("dp", "mp"), None),
        P(("dp", "mp"), None),
        P(("dp", "mp"), None, None),
        P(("dp", "mp"), None),
        P(("dp", "mp"), None),
        P(None, "mp"),
        P("mp", None),
    )
    return jax.shard_map(
        on_device, mesh=mesh, in_specs=in_specs, out_specs=out_specs, check_vma=False
    )
```

profile of v0, /device:TPU:0, one launch (start us, length us, event | category | flops | bytes accessed | tf_op | source)
XLA Modules:
  0.0 1150.4 jit_solution(354318930607846485)
XLA Ops:
  11.2 69.5 %all-gather = bf16[32,24,2]{1,2,0:T(2,128)(2,1)S(1)} all-gather(bf16[1,24,2]{1,2,0:T(2,128)(2,1)} %bitcast.223), channel_id=1, replica_groups=mesh['dp'=4,'mp'=8] {'dp','mp'}, dimensions={0}, use_global_device_ids=true | all-gather | bytes 3168 | tf_op jit(solution)/shard_map/all_gather | solution.py:101
  80.7 63.2 %all-gather.1 = bf16[32,24,2]{1,2,0:T(2,128)(2,1)S(1)} all-gather(bf16[1,24,2]{1,2,0:T(2,128)(2,1)} %bitcast.224), channel_id=1, replica_groups=mesh['dp'=4,'mp'=8] {'dp','mp'}, dimensions={0}, use_global_device_ids=true | all-gather | bytes 3168 | tf_op jit(solution)/shard_map/all_gather | solution.py:102
  145.3 70.3 %all_gather.24 = bf16[768,3,3]{2,1,0:T(4,128)(2,1)S(1)} all-gather(bf16[24,3,3]{2,1,0:T(4,128)(2,1)S(1)} %copy.74), channel_id=1, replica_groups=mesh['dp'=4,'mp'=8] {'dp','mp'}, dimensions={0}, use_global_device_ids=true | all-gather | bytes 14256 | tf_op jit(solution)/shard_map/all_gather | solution.py:100
  235.2 147.4 %while.84 = (s32[]{:T(128)}, bf16[256,1536]{1,0:T(8,128)(2,1)S(1)}, bf16[2048,1536]{1,0:T(8,128)(2,1)}, s32[]{:T(128)}, s32[]{:T(128)}, /*index=5*/s32[]{:T(128)}, s32[]{:T(128)}, s32[]{:T(128)}) while((s32[]{:T(128)}, bf16[256,1536]{1,0:T(8,128)(2,1)S(1)}, bf16[2048,1536]{1,0:T(8,128)(2,1)}, s32[]{:T(128)}, s32[]{:T(128)}, ...), condition=%wide.region_3.4_spmd, body=%wide.region_2.3_spmd.sunk | while | flops 7 | bytes 6291643 | solution.py:133
  239.4 15.3 %collective-permute-done = bf16[256,1536]{1,0:T(8,128)(2,1)S(1)} collective-permute-done((bf16[256,1536]{1,0:T(8,128)(2,1)S(1)}, bf16[256,1536]{1,0:T(8,128)(2,1)S(1)}, u32[]{:S(2)}, u32[]{:S(2)}) %collective-permute-start) | collective-permute-done | bytes 786464 | tf_op jit(solution)/shard_map/while/body/eval_jaxpr/ppermute | solution.py:13
  260.1 16.4 %collective-permute-done = bf16[256,1536]{1,0:T(8,128)(2,1)S(1)} collective-permute-done((bf16[256,1536]{1,0:T(8,128)(2,1)S(1)}, bf16[256,1536]{1,0:T(8,128)(2,1)S(1)}, u32[]{:S(2)}, u32[]{:S(2)}) %collective-permute-start) | collective-permute-done | bytes 786464 | tf_op jit(solution)/shard_map/while/body/eval_jaxpr/ppermute | solution.py:13
  282.0 17.5 %collective-permute-done = bf16[256,1536]{1,0:T(8,128)(2,1)S(1)} collective-permute-done((bf16[256,1536]{1,0:T(8,128)(2,1)S(1)}, bf16[256,1536]{1,0:T(8,128)(2,1)S(1)}, u32[]{:S(2)}, u32[]{:S(2)}) %collective-permute-start) | collective-permute-done | bytes 786464 | tf_op jit(solution)/shard_map/while/body/eval_jaxpr/ppermute | solution.py:13
  304.9 17.0 %collective-permute-done = bf16[256,1536]{1,0:T(8,128)(2,1)S(1)} collective-permute-done((bf16[256,1536]{1,0:T(8,128)(2,1)S(1)}, bf16[256,1536]{1,0:T(8,128)(2,1)S(1)}, u32[]{:S(2)}, u32[]{:S(2)}) %collective-permute-start) | collective-permute-done | bytes 786464 | tf_op jit(solution)/shard_map/while/body/eval_jaxpr/ppermute | solution.py:13
  327.4 16.2 %collective-permute-done = bf16[256,1536]{1,0:T(8,128)(2,1)S(1)} collective-permute-done((bf16[256,1536]{1,0:T(8,128)(2,1)S(1)}, bf16[256,1536]{1,0:T(8,128)(2,1)S(1)}, u32[]{:S(2)}, u32[]{:S(2)}) %collective-permute-start) | collective-permute-done | bytes 786464 | tf_op jit(solution)/shard_map/while/body/eval_jaxpr/ppermute | solution.py:13
  349.1 16.8 %collective-permute-done = bf16[256,1536]{1,0:T(8,128)(2,1)S(1)} collective-permute-done((bf16[256,1536]{1,0:T(8,128)(2,1)S(1)}, bf16[256,1536]{1,0:T(8,128)(2,1)S(1)}, u32[]{:S(2)}, u32[]{:S(2)}) %collective-permute-start) | collective-permute-done | bytes 786464 | tf_op jit(solution)/shard_map/while/body/eval_jaxpr/ppermute | solution.py:13
  366.9 5.2 collective-permute-start
  372.1 9.4 collective-permute-done
  382.5 8.6 copy.78
  400.8 97.2 %all-gather.11.cloned.1.call-done = bf16[2048,768]{1,0:T(8,128)(2,1)} async-done(((bf16[256,768]{1,0:T(8,128)(2,1)}), bf16[2048,768]{1,0:T(8,128)(2,1)}) %all-gather.11.cloned.1.call-update) | async-done | bytes 3145744 | tf_op jit(solution)/shard_map/all_gather | solution.py:192
  498.1 5.4 convolution_maximum_fusion
  503.4 55.8 %all-gather.13.cloned.1.call-done = bf16[2048,768]{1,0:T(8,128)(2,1)} async-done(((bf16[256,768]{1,0:T(8,128)(2,1)}), bf16[2048,768]{1,0:T(8,128)(2,1)}) %all-gather.13.cloned.1.call-update) | async-done | bytes 3145744 | tf_op jit(solution)/shard_map/all_gather | solution.py:202
  568.6 5.4 convolution_convert_fusion.1
  583.2 57.6 %reduce-scatter.10.cloned.1.call-done = bf16[256,768]{1,0:T(8,128)(2,1)} async-done(((bf16[2048,768]{1,0:T(8,128)(2,1)}), bf16[256,768]{1,0:T(8,128)(2,1)}) %reduce-scatter.10.cloned.1.call-update) | async-done | bytes 393232 | tf_op jit(solution)/shard_map/reduce_scatter | solution.py:207
  642.2 75.6 %reduce-scatter.8.cloned.1.call-done = bf16[256,768]{1,0:T(8,128)(2,1)} async-done(((bf16[2048,768]{1,0:T(8,128)(2,1)}), bf16[256,768]{1,0:T(8,128)(2,1)}) %reduce-scatter.8.cloned.1.call-update) | async-done | bytes 393232 | tf_op jit(solution)/shard_map/reduce_scatter | solution.py:195
  725.8 6.2 broadcast_in_dim.195
  732.0 8.1 while.89
  746.4 249.6 %while.85 = (s32[]{:T(128)}, f32[256,1536]{1,0:T(8,128)}, f32[2048,1536]{0,1:T(8,128)}, s32[]{:T(128)}, s32[]{:T(128)}, /*index=5*/s32[]{:T(128)}, s32[]{:T(128)}, s32[]{:T(128)}, s32[]{:T(128)}) while((s32[]{:T(128)}, f32[256,1536]{1,0:T(8,128)}, f32[2048,1536]{0,1:T(8,128)}, s32[]{:T(128)}, s32[]{:T(128)}, /*index=5*/s32[]{:T(128)}, ...), condition=%wide.region_22.23_spmd, body=%wide.region_21.22_spmd.sunk | while | flops 1179656 | bytes 15728847 | solution.py:273
  752.1 28.8 %collective-permute-done.1 = bf16[256,1536]{1,0:T(8,128)(2,1)} collective-permute-done((bf16[256,1536]{1,0:T(8,128)(2,1)}, bf16[256,1536]{1,0:T(8,128)(2,1)}, u32[]{:S(2)}, u32[]{:S(2)}) %collective-permute-start.1) | collective-permute-done | bytes 786464 | tf_op jit(solution)/shard_map/while/body/eval_jaxpr/ppermute | solution.py:13
  789.0 27.7 %collective-permute-done.1 = bf16[256,1536]{1,0:T(8,128)(2,1)} collective-permute-done((bf16[256,1536]{1,0:T(8,128)(2,1)}, bf16[256,1536]{1,0:T(8,128)(2,1)}, u32[]{:S(2)}, u32[]{:S(2)}) %collective-permute-start.1) | collective-permute-done | bytes 786464 | tf_op jit(solution)/shard_map/while/body/eval_jaxpr/ppermute | solution.py:13
  824.9 28.6 %collective-permute-done.1 = bf16[256,1536]{1,0:T(8,128)(2,1)} collective-permute-done((bf16[256,1536]{1,0:T(8,128)(2,1)}, bf16[256,1536]{1,0:T(8,128)(2,1)}, u32[]{:S(2)}, u32[]{:S(2)}) %collective-permute-start.1) | collective-permute-done | bytes 786464 | tf_op jit(solution)/shard_map/while/body/eval_jaxpr/ppermute | solution.py:13
  861.8 29.4 %collective-permute-done.1 = bf16[256,1536]{1,0:T(8,128)(2,1)} collective-permute-done((bf16[256,1536]{1,0:T(8,128)(2,1)}, bf16[256,1536]{1,0:T(8,128)(2,1)}, u32[]{:S(2)}, u32[]{:S(2)}) %collective-permute-start.1) | collective-permute-done | bytes 786464 | tf_op jit(solution)/shard_map/while/body/eval_jaxpr/ppermute | solution.py:13
  899.3 28.2 %collective-permute-done.1 = bf16[256,1536]{1,0:T(8,128)(2,1)} collective-permute-done((bf16[256,1536]{1,0:T(8,128)(2,1)}, bf16[256,1536]{1,0:T(8,128)(2,1)}, u32[]{:S(2)}, u32[]{:S(2)}) %collective-permute-start.1) | collective-permute-done | bytes 786464 | tf_op jit(solution)/shard_map/while/body/eval_jaxpr/ppermute | solution.py:13
  935.7 28.3 %collective-permute-done.1 = bf16[256,1536]{1,0:T(8,128)(2,1)} collective-permute-done((bf16[256,1536]{1,0:T(8,128)(2,1)}, bf16[256,1536]{1,0:T(8,128)(2,1)}, u32[]{:S(2)}, u32[]{:S(2)}) %collective-permute-start.1) | collective-permute-done | bytes 786464 | tf_op jit(solution)/shard_map/while/body/eval_jaxpr/ppermute | solution.py:13
  972.2 21.2 %collective-permute-done.1 = bf16[256,1536]{1,0:T(8,128)(2,1)} collective-permute-done((bf16[256,1536]{1,0:T(8,128)(2,1)}, bf16[256,1536]{1,0:T(8,128)(2,1)}, u32[]{:S(2)}, u32[]{:S(2)}) %collective-permute-start.1) | collective-permute-done | bytes 786464 | tf_op jit(solution)/shard_map/while/body/eval_jaxpr/ppermute | solution.py:13
  998.4 6.6 collective-permute-done.3
  1021.8 50.3 %all-reduce.4 = (f32[768,3,3]{0,2,1:T(4,128)S(1)}, f32[768,2]{0,1:T(2,128)S(1)}, f32[768,2]{0,1:T(2,128)S(1)}) all-reduce(f32[768,3,3]{0,2,1:T(4,128)S(1)} %maximum_bitcast_fusion, f32[768,2]{0,1:T(2,128)S(1)} %pad_maximum_fusion.3, f32[768,2]{0,1:T(2,128)S(1)} %pad_maximum_fusion.4), channel_id=6, replica_groups=mesh['dp'=4,'mp'=8] {'dp','mp'}, use_global_device_ids=true, to_apply=%region_30.31.clone | all-reduce | flops 9984 | bytes 79872
  1076.4 67.4 %reduce-scatter.12.cloned.1.call-done = f32[24,2304]{1,0:T(8,128)} async-done(((f32[768,2304]{1,0:T(8,128)}), f32[24,2304]{1,0:T(8,128)}) %reduce-scatter.12.cloned.1.call-update) | async-done | bytes 221200 | tf_op jit(solution)/shard_map/reduce_scatter | solution.py:288
  (241 shorter events, 198.9 us)
Async XLA Ops:
  7.2 490.9 %copy-start = (bf16[768,384]{1,0:T(8,128)(2,1)S(1)}, bf16[768,384]{1,0:T(8,128)(2,1)}, u32[]{:S(2)}) copy-start(bf16[768,384]{1,0:T(8,128)(2,1)} %param.29) | copy-start | bytes 1769476
  7.2 211.6 %copy-start.5 = (bf16[256,768]{1,0:T(8,128)(2,1)S(1)}, bf16[256,768]{1,0:T(8,128)(2,1)}, u32[]{:S(2)}) copy-start(bf16[256,768]{1,0:T(8,128)(2,1)} %param.22) | copy-start | bytes 1179652
  7.2 211.3 %copy-start.16 = (s32[2048]{0:T(1024)S(1)}, s32[2048]{0:T(1024)}, u32[]{:S(2)}) copy-start(s32[2048]{0:T(1024)} %param.23) | copy-start | bytes 24580
  7.2 211.6 %all-gather.7.cloned.1.call-start = ((), (), s32[]{:S(2)}) async-start(), calls=%async_computation.4 | async-start | bytes 3649536 | tf_op jit(solution)/shard_map/all_gather | solution.py:98
  7.9 388.9 %all-gather.9.cloned.1.call-start = ((), (), s32[]{:S(2)}) async-start(), calls=%async_computation.5 | async-start | bytes 1216512 | tf_op jit(solution)/shard_map/all_gather | solution.py:99
  8.7 489.4 %all-gather.11.cloned.1.call-start = ((), (), s32[]{:S(2)}) async-start(), calls=%async_computation.6 | async-start | bytes 3538944 | tf_op jit(solution)/shard_map/all_gather | solution.py:192
  9.9 212.1 %copy-start.19 = (f32[256]{0:T(256)}, f32[256]{0:T(256)S(1)}, u32[]{:S(2)}) copy-start(f32[256]{0:T(256)S(1)} %broadcast_multiply_fusion.5) | copy-start | bytes 3076
  11.2 210.9 %copy-start.21 = (f32[256]{0:T(256)}, f32[256]{0:T(256)S(1)}, u32[]{:S(2)}) copy-start(f32[256]{0:T(256)S(1)} %add_rsqrt_fusion.1) | copy-start | bytes 3076
  223.5 3.8 collective-permute-start.2
  235.2 19.5 %collective-permute-start = (bf16[256,1536]{1,0:T(8,128)(2,1)S(1)}, bf16[256,1536]{1,0:T(8,128)(2,1)S(1)}, u32[]{:S(2)}, u32[]{:S(2)}) collective-permute-start(bf16[256,1536]{1,0:T(8,128)(2,1)S(1)} %get-tuple-element.1378), channel_id=1, source_target_pairs={{0,1},{1,2},{2,3},{3,4},{4,5},{5,6},{6,7},{8,9},{9,10},{10,11},{11... | collective-permute-start | bytes 2359304 | tf_op jit(solution)/shard_map/while/body/eval_jaxpr/ppermute | solution.py:13
  255.7 20.8 %collective-permute-start = (bf16[256,1536]{1,0:T(8,128)(2,1)S(1)}, bf16[256,1536]{1,0:T(8,128)(2,1)S(1)}, u32[]{:S(2)}, u32[]{:S(2)}) collective-permute-start(bf16[256,1536]{1,0:T(8,128)(2,1)S(1)} %get-tuple-element.1378), channel_id=1, source_target_pairs={{0,1},{1,2},{2,3},{3,4},{4,5},{5,6},{6,7},{8,9},{9,10},{10,11},{11... | collective-permute-start | bytes 2359304 | tf_op jit(solution)/shard_map/while/body/eval_jaxpr/ppermute | solution.py:13
  277.5 22.0 %collective-permute-start = (bf16[256,1536]{1,0:T(8,128)(2,1)S(1)}, bf16[256,1536]{1,0:T(8,128)(2,1)S(1)}, u32[]{:S(2)}, u32[]{:S(2)}) collective-permute-start(bf16[256,1536]{1,0:T(8,128)(2,1)S(1)} %get-tuple-element.1378), channel_id=1, source_target_pairs={{0,1},{1,2},{2,3},{3,4},{4,5},{5,6},{6,7},{8,9},{9,10},{10,11},{11... | collective-permute-start | bytes 2359304 | tf_op jit(solution)/shard_map/while/body/eval_jaxpr/ppermute | solution.py:13
  300.5 21.5 %collective-permute-start = (bf16[256,1536]{1,0:T(8,128)(2,1)S(1)}, bf16[256,1536]{1,0:T(8,128)(2,1)S(1)}, u32[]{:S(2)}, u32[]{:S(2)}) collective-permute-start(bf16[256,1536]{1,0:T(8,128)(2,1)S(1)} %get-tuple-element.1378), channel_id=1, source_target_pairs={{0,1},{1,2},{2,3},{3,4},{4,5},{5,6},{6,7},{8,9},{9,10},{10,11},{11... | collective-permute-start | bytes 2359304 | tf_op jit(solution)/shard_map/while/body/eval_jaxpr/ppermute | solution.py:13
  323.0 20.6 %collective-permute-start = (bf16[256,1536]{1,0:T(8,128)(2,1)S(1)}, bf16[256,1536]{1,0:T(8,128)(2,1)S(1)}, u32[]{:S(2)}, u32[]{:S(2)}) collective-permute-start(bf16[256,1536]{1,0:T(8,128)(2,1)S(1)} %get-tuple-element.1378), channel_id=1, source_target_pairs={{0,1},{1,2},{2,3},{3,4},{4,5},{5,6},{6,7},{8,9},{9,10},{10,11},{11... | collective-permute-start | bytes 2359304 | tf_op jit(solution)/shard_map/while/body/eval_jaxpr/ppermute | solution.py:13
  344.6 21.2 %collective-permute-start = (bf16[256,1536]{1,0:T(8,128)(2,1)S(1)}, bf16[256,1536]{1,0:T(8,128)(2,1)S(1)}, u32[]{:S(2)}, u32[]{:S(2)}) collective-permute-start(bf16[256,1536]{1,0:T(8,128)(2,1)S(1)} %get-tuple-element.1378), channel_id=1, source_target_pairs={{0,1},{1,2},{2,3},{3,4},{4,5},{5,6},{6,7},{8,9},{9,10},{10,11},{11... | collective-permute-start | bytes 2359304 | tf_op jit(solution)/shard_map/while/body/eval_jaxpr/ppermute | solution.py:13
  366.9 14.7 %collective-permute-start = (bf16[256,1536]{1,0:T(8,128)(2,1)S(1)}, bf16[256,1536]{1,0:T(8,128)(2,1)S(1)}, u32[]{:S(2)}, u32[]{:S(2)}) collective-permute-start(bf16[256,1536]{1,0:T(8,128)(2,1)S(1)} %get-tuple-element.1378), channel_id=1, source_target_pairs={{0,1},{1,2},{2,3},{3,4},{4,5},{5,6},{6,7},{8,9},{9,10},{10,11},{11... | collective-permute-start | bytes 2359304 | tf_op jit(solution)/shard_map/while/body/eval_jaxpr/ppermute | solution.py:13
  400.0 159.2 %all-gather.13.cloned.1.call-start = ((), (), s32[]{:S(2)}) async-start(), calls=%async_computation.8 | async-start | bytes 3538944 | tf_op jit(solution)/shard_map/all_gather | solution.py:202
  400.6 240.2 %reduce-scatter.10.cloned.1.call-start = ((), (), s32[]{:S(2)}) async-start(), calls=%async_computation.9 | async-start | bytes 3538944 | tf_op jit(solution)/shard_map/reduce_scatter | solution.py:207
  567.6 150.2 %reduce-scatter.8.cloned.1.call-start = ((), (), s32[]{:S(2)}) async-start(), calls=%async_computation.7 | async-start | bytes 3538944 | tf_op jit(solution)/shard_map/reduce_scatter | solution.py:195
  574.0 441.0 %all-reduce.8.cloned.1.call-start = ((), (), s32[]{:S(2)}) async-start(), calls=%async_computation.12 | async-start | bytes 2359296 | tf_op jit(solution)/shard_map/psum | solution.py:211
  578.8 139.1 %copy-start.13 = (bf16[256,768]{1,0:T(8,128)(2,1)S(1)}, bf16[256,768]{1,0:T(8,128)(2,1)}, u32[]{:S(2)}) copy-start(bf16[256,768]{1,0:T(8,128)(2,1)} %param.31) | copy-start | bytes 1179652
  583.2 493.3 %reduce-scatter.14.cloned.1.call-start = ((), (), s32[]{:S(2)}) async-start(), calls=%async_computation.11 | async-start | bytes 2433024 | tf_op jit(solution)/shard_map/reduce_scatter | solution.py:289
  746.3 397.5 %reduce-scatter.12.cloned.1.call-start = ((), (), s32[]{:S(2)}) async-start(), calls=%async_computation.10 | async-start | bytes 7299072 | tf_op jit(solution)/shard_map/reduce_scatter | solution.py:288
  748.8 32.0 %collective-permute-start.1 = (bf16[256,1536]{1,0:T(8,128)(2,1)}, bf16[256,1536]{1,0:T(8,128)(2,1)}, u32[]{:S(2)}, u32[]{:S(2)}) collective-permute-start(bf16[256,1536]{1,0:T(8,128)(2,1)} %convert_element_type.230), channel_id=1, source_target_pairs={{1,0},{2,1},{3,2},{4,3},{5,4},{6,5},{7,6},{9,8},{10,9},{11,10},{12... | collective-permute-start | bytes 2359304 | tf_op jit(solution)/shard_map/while/body/eval_jaxpr/ppermute | solution.py:13
  785.7 31.0 %collective-permute-start.1 = (bf16[256,1536]{1,0:T(8,128)(2,1)}, bf16[256,1536]{1,0:T(8,128)(2,1)}, u32[]{:S(2)}, u32[]{:S(2)}) collective-permute-start(bf16[256,1536]{1,0:T(8,128)(2,1)} %convert_element_type.230), channel_id=1, source_target_pairs={{1,0},{2,1},{3,2},{4,3},{5,4},{6,5},{7,6},{9,8},{10,9},{11,10},{12... | collective-permute-start | bytes 2359304 | tf_op jit(solution)/shard_map/while/body/eval_jaxpr/ppermute | solution.py:13
  821.6 31.9 %collective-permute-start.1 = (bf16[256,1536]{1,0:T(8,128)(2,1)}, bf16[256,1536]{1,0:T(8,128)(2,1)}, u32[]{:S(2)}, u32[]{:S(2)}) collective-permute-start(bf16[256,1536]{1,0:T(8,128)(2,1)} %convert_element_type.230), channel_id=1, source_target_pairs={{1,0},{2,1},{3,2},{4,3},{5,4},{6,5},{7,6},{9,8},{10,9},{11,10},{12... | collective-permute-start | bytes 2359304 | tf_op jit(solution)/shard_map/while/body/eval_jaxpr/ppermute | solution.py:13
  858.4 32.7 %collective-permute-start.1 = (bf16[256,1536]{1,0:T(8,128)(2,1)}, bf16[256,1536]{1,0:T(8,128)(2,1)}, u32[]{:S(2)}, u32[]{:S(2)}) collective-permute-start(bf16[256,1536]{1,0:T(8,128)(2,1)} %convert_element_type.230), channel_id=1, source_target_pairs={{1,0},{2,1},{3,2},{4,3},{5,4},{6,5},{7,6},{9,8},{10,9},{11,10},{12... | collective-permute-start | bytes 2359304 | tf_op jit(solution)/shard_map/while/body/eval_jaxpr/ppermute | solution.py:13
  896.0 31.5 %collective-permute-start.1 = (bf16[256,1536]{1,0:T(8,128)(2,1)}, bf16[256,1536]{1,0:T(8,128)(2,1)}, u32[]{:S(2)}, u32[]{:S(2)}) collective-permute-start(bf16[256,1536]{1,0:T(8,128)(2,1)} %convert_element_type.230), channel_id=1, source_target_pairs={{1,0},{2,1},{3,2},{4,3},{5,4},{6,5},{7,6},{9,8},{10,9},{11,10},{12... | collective-permute-start | bytes 2359304 | tf_op jit(solution)/shard_map/while/body/eval_jaxpr/ppermute | solution.py:13
  932.4 31.6 %collective-permute-start.1 = (bf16[256,1536]{1,0:T(8,128)(2,1)}, bf16[256,1536]{1,0:T(8,128)(2,1)}, u32[]{:S(2)}, u32[]{:S(2)}) collective-permute-start(bf16[256,1536]{1,0:T(8,128)(2,1)} %convert_element_type.230), channel_id=1, source_target_pairs={{1,0},{2,1},{3,2},{4,3},{5,4},{6,5},{7,6},{9,8},{10,9},{11,10},{12... | collective-permute-start | bytes 2359304 | tf_op jit(solution)/shard_map/while/body/eval_jaxpr/ppermute | solution.py:13
  968.9 24.5 %collective-permute-start.1 = (bf16[256,1536]{1,0:T(8,128)(2,1)}, bf16[256,1536]{1,0:T(8,128)(2,1)}, u32[]{:S(2)}, u32[]{:S(2)}) collective-permute-start(bf16[256,1536]{1,0:T(8,128)(2,1)} %convert_element_type.230), channel_id=1, source_target_pairs={{1,0},{2,1},{3,2},{4,3},{5,4},{6,5},{7,6},{9,8},{10,9},{11,10},{12... | collective-permute-start | bytes 2359304 | tf_op jit(solution)/shard_map/while/body/eval_jaxpr/ppermute | solution.py:13
  996.9 8.1 collective-permute-start.3
  1019.6 124.3 %copy-start.1 = (bf16[768,384]{1,0:T(8,128)(2,1)S(1)}, bf16[768,384]{1,0:T(8,128)(2,1)}, u32[]{:S(2)}) copy-start(bf16[768,384]{1,0:T(8,128)(2,1)} %param.29) | copy-start | bytes 1769476
  (17 other events, 397.8 us)
Sparse Core Ops, SparseCore 0:
  11.0 62.9 all-gather.6
  77.1 52.9 all-gather.8
  400.1 97.8 all-gather.10
  500.1 59.0 all-gather.12
  567.7 73.0 reduce-scatter.9
  644.2 73.5 reduce-scatter.7
  720.2 36.7 all-reduce.7
  762.9 164.5 reduce-scatter.13
  1015.2 128.6 reduce-scatter.11
where the time goes:
time: 1150 us
  waiting for transfers between devices  664 us (58%)
  blocking collectives  253 us (22%)
  other arithmetic  65.3 us (6%)
  local copies, waits for them, and re-layouts  56.3 us (5%)
  matrix products  51 us (4%)
  starting transfers between devices  44.8 us (4%)
  between operations  14.5 us (1%)
    ppermute x16, waiting for transfers between devices, from_behind(): lax.ppermute(value, axis, [(source, source + steps) for source in range(l...  309 us
    all_gather x1, waiting for transfers between devices, on_device(): normed2_rows = lax.all_gather(normed2, 'mp', axis=0, tiled=True)  97.2 us
    reduce_scatter x1, waiting for transfers between devices, on_device(): lax.psum_scatter(jnp.dot(hidden, w_down, preferred_element_type=jnp.float...  75.6 us
    all_gather x1, blocking collectives, on_device(): lax.all_gather(conv_taps, ('dp', 'mp'), axis=0, tiled=True)  70.3 us
    all_gather x1, blocking collectives, on_device(): lax.all_gather(norm_gain, ('dp', 'mp'), axis=0, tiled=True)  69.5 us
    reduce_scatter x1, waiting for transfers between devices, on_device(): lax.psum_scatter(qkv_local, ('dp', 'mp'), scatter_dimension=0, tiled=True)  67.4 us
    all_gather x1, blocking collectives, on_device(): lax.all_gather(norm_bias, ('dp', 'mp'), axis=0, tiled=True)  63.2 us
    reduce_scatter x1, waiting for transfers between devices, on_device(): lax.psum_scatter(contract_last(upper_grad, w_up).astype(jnp.bfloat16), 'm...  57.6 us
  transfers between devices with their start and end apart: 25, of which 21 were waited for; matrix products, arithmetic and copies ran while one was open for 14% of the time, Pallas kernels for 0%

commit v1 on v0

--- a/solution.py
+++ b/solution.py
@@ -5,6 +5,12 @@
 
 HEAD_DIM = 64
 eps_norm = 1e-05
+
+
+def in_order(tiles, dim):
+    tiles = jnp.moveaxis(tiles, 0, dim)
+    dims = tiles.shape
+    return tiles.reshape(*dims[:dim], dims[dim] * dims[dim + 1], *dims[dim + 2 :])
 
 
 def from_behind(value, axis, steps):
@@ -189,7 +195,19 @@
     residual = inputs + mixed
     normed2_full, normal2, inverse2 = layer_norm(residual, gains[:, 1], biases[:, 1])
     normed2 = normed2_full.astype(jnp.bfloat16)
-    normed2_rows = lax.all_gather(normed2, "mp", axis=0, tiled=True)
+    size = lax.axis_size("mp")
+    pairs = [(i, (i + 1) % size) for i in range(size)]
+    back = [(b, a) for a, b in pairs]
+    lower, upper_2 = ([], [])
+    for step_2 in range(size - 1):
+        if step_2 % 2 == 0:
+            lower.append(lax.ppermute(lower[-1] if lower else normed2, "mp", pairs))
+        else:
+            upper_2.append(lax.ppermute(upper_2[-1] if upper_2 else normed2, "mp", back))
+    blocks = jnp.stack([*lower[::-1], normed2, *upper_2])
+    shift = lax.axis_index("mp") - len(lower)
+    blocks = blocks[(jnp.arange(size) - shift) % size]
+    normed2_rows = in_order(blocks, 0)
     upper = jnp.dot(normed2_rows, w_up, preferred_element_type=jnp.float32)
     hidden = jnp.square(jnp.maximum(upper, 0.0)).astype(jnp.bfloat16)
     ff_out = lax.psum_scatter(

time: 1150 us -> 1110 us (0.965)
  waiting for transfers between devices: 664 us -> 563 us
  starting transfers between devices: 44.8 us -> 88.1 us
  local copies, waits for them, and re-layouts: 56.3 us -> 69.1 us
    all_gather x1 -> x0, waiting for transfers between devices: 97.2 us -> none  [on_device(): normed2_rows = lax.all_gather(normed2, 'mp', axis=0, tiled=True)]
    all_gather x1, waiting for transfers between devices: 55.8 us -> 0.01 us  [on_device(): grad_all = lax.all_gather(out_grad, 'mp', axis=0, tiled=True)]
    ppermute x0 -> x7, waiting for transfers between devices: none -> 54.1 us  [the longest x4 49.1 us: on_device(): lower.append(lax.ppermute(lower[-1] if lower else normed2, 'mp', pairs))]
    ppermute x0 -> x7, starting transfers between devices: none -> 42.9 us  [the longest x3 32.3 us: on_device(): lax.ppermute(upper_2[-1] if upper_2 else normed2, 'mp', back)]
  transfers between devices with their start and end apart: 25 -> 31, of which waited for: 21 -> 25; matrix products, arithmetic and copies ran while one was open for 14% -> 16% of each run, Pallas kernels for 0% -> 0%
where the time goes in v1:
time: 1110 us; the launch traced here: 1100 us
  waiting for transfers between devices  563 us (51%)
  blocking collectives  252 us (23%)
  starting transfers between devices  88.1 us (8%)
  local copies, waits for them, and re-layouts  69.1 us (6%)
  other arithmetic  66.1 us (6%)
  matrix products  50.9 us (5%)
  between operations  14.8 us (1%)
    ppermute x16, waiting for transfers between devices, from_behind(): lax.ppermute(value, axis, [(source, source + steps) for source in range(l...  304 us
    reduce_scatter x1, waiting for transfers between devices, on_device(): lax.psum_scatter(jnp.dot(hidden, w_down, preferred_element_type=jnp.float...  75.6 us
    all_gather x1, blocking collectives, on_device(): lax.all_gather(conv_taps, ('dp', 'mp'), axis=0, tiled=True)  72.8 us
    all_gather x1, blocking collectives, on_device(): lax.all_gather(norm_gain, ('dp', 'mp'), axis=0, tiled=True)  69.5 us
    reduce_scatter x1, waiting for transfers between devices, on_device(): lax.psum_scatter(qkv_local, ('dp', 'mp'), scatter_dimension=0, tiled=True)  67.4 us
    all_gather x1, blocking collectives, on_device(): lax.all_gather(norm_bias, ('dp', 'mp'), axis=0, tiled=True)  63.2 us
    reduce_scatter x1, waiting for transfers between devices, on_device(): lax.psum_scatter(contract_last(upper_grad, w_up).astype(jnp.bfloat16), 'm...  60.3 us
    ppermute x4, waiting for transfers between devices, on_device(): lower.append(lax.ppermute(lower[-1] if lower else normed2, 'mp', pairs))  49.1 us
  transfers between devices with their start and end apart: 31, of which 25 were waited for; matrix products, arithmetic and copies ran while one was open for 16% of the time, Pallas kernels for 0%

profile of v1, /device:TPU:0, one launch (start us, length us, event | category | flops | bytes accessed | tf_op | source)
XLA Modules:
  0.0 1104.5 jit_solution(166072159114283777)
XLA Ops:
  11.9 69.5 %all-gather = bf16[32,24,2]{1,2,0:T(2,128)(2,1)S(1)} all-gather(bf16[1,24,2]{1,2,0:T(2,128)(2,1)} %bitcast.244), channel_id=1, replica_groups=mesh['dp'=4,'mp'=8] {'dp','mp'}, dimensions={0}, use_global_device_ids=true | all-gather | bytes 3168 | tf_op jit(solution)/shard_map/all_gather | solution.py:107
  81.5 63.2 %all-gather.1 = bf16[32,24,2]{1,2,0:T(2,128)(2,1)S(1)} all-gather(bf16[1,24,2]{1,2,0:T(2,128)(2,1)} %bitcast.245), channel_id=1, replica_groups=mesh['dp'=4,'mp'=8] {'dp','mp'}, dimensions={0}, use_global_device_ids=true | all-gather | bytes 3168 | tf_op jit(solution)/shard_map/all_gather | solution.py:108
  146.0 72.8 %all_gather.21 = bf16[768,3,3]{2,1,0:T(4,128)(2,1)S(1)} all-gather(bf16[24,3,3]{2,1,0:T(4,128)(2,1)S(1)} %copy.74), channel_id=1, replica_groups=mesh['dp'=4,'mp'=8] {'dp','mp'}, dimensions={0}, use_global_device_ids=true | all-gather | bytes 14256 | tf_op jit(solution)/shard_map/all_gather | solution.py:106
  240.0 143.8 %while.84 = (s32[]{:T(128)}, bf16[256,1536]{1,0:T(8,128)(2,1)S(1)}, bf16[2048,1536]{1,0:T(8,128)(2,1)}, s32[]{:T(128)}, s32[]{:T(128)}, /*index=5*/s32[]{:T(128)}, s32[]{:T(128)}, s32[]{:T(128)}) while((s32[]{:T(128)}, bf16[256,1536]{1,0:T(8,128)(2,1)S(1)}, bf16[2048,1536]{1,0:T(8,128)(2,1)}, s32[]{:T(128)}, s32[]{:T(128)}, ...), condition=%wide.region_3.4_spmd, body=%wide.region_2.3_spmd.sunk | while | flops 7 | bytes 6291643 | solution.py:139
  244.3 14.1 %collective-permute-done = bf16[256,1536]{1,0:T(8,128)(2,1)S(1)} collective-permute-done((bf16[256,1536]{1,0:T(8,128)(2,1)S(1)}, bf16[256,1536]{1,0:T(8,128)(2,1)S(1)}, u32[]{:S(2)}, u32[]{:S(2)}) %collective-permute-start) | collective-permute-done | bytes 786464 | tf_op jit(solution)/shard_map/while/body/eval_jaxpr/ppermute | solution.py:19
  263.8 15.2 %collective-permute-done = bf16[256,1536]{1,0:T(8,128)(2,1)S(1)} collective-permute-done((bf16[256,1536]{1,0:T(8,128)(2,1)S(1)}, bf16[256,1536]{1,0:T(8,128)(2,1)S(1)}, u32[]{:S(2)}, u32[]{:S(2)}) %collective-permute-start) | collective-permute-done | bytes 786464 | tf_op jit(solution)/shard_map/while/body/eval_jaxpr/ppermute | solution.py:19
  284.5 16.3 %collective-permute-done = bf16[256,1536]{1,0:T(8,128)(2,1)S(1)} collective-permute-done((bf16[256,1536]{1,0:T(8,128)(2,1)S(1)}, bf16[256,1536]{1,0:T(8,128)(2,1)S(1)}, u32[]{:S(2)}, u32[]{:S(2)}) %collective-permute-start) | collective-permute-done | bytes 786464 | tf_op jit(solution)/shard_map/while/body/eval_jaxpr/ppermute | solution.py:19
  306.3 17.5 %collective-permute-done = bf16[256,1536]{1,0:T(8,128)(2,1)S(1)} collective-permute-done((bf16[256,1536]{1,0:T(8,128)(2,1)S(1)}, bf16[256,1536]{1,0:T(8,128)(2,1)S(1)}, u32[]{:S(2)}, u32[]{:S(2)}) %collective-permute-start) | collective-permute-done | bytes 786464 | tf_op jit(solution)/shard_map/while/body/eval_jaxpr/ppermute | solution.py:19
  329.3 17.0 %collective-permute-done = bf16[256,1536]{1,0:T(8,128)(2,1)S(1)} collective-permute-done((bf16[256,1536]{1,0:T(8,128)(2,1)S(1)}, bf16[256,1536]{1,0:T(8,128)(2,1)S(1)}, u32[]{:S(2)}, u32[]{:S(2)}) %collective-permute-start) | collective-permute-done | bytes 786464 | tf_op jit(solution)/shard_map/while/body/eval_jaxpr/ppermute | solution.py:19
  351.7 16.2 %collective-permute-done = bf16[256,1536]{1,0:T(8,128)(2,1)S(1)} collective-permute-done((bf16[256,1536]{1,0:T(8,128)(2,1)S(1)}, bf16[256,1536]{1,0:T(8,128)(2,1)S(1)}, u32[]{:S(2)}, u32[]{:S(2)}) %collective-permute-start) | collective-permute-done | bytes 786464 | tf_op jit(solution)/shard_map/while/body/eval_jaxpr/ppermute | solution.py:19
  373.4 9.4 collective-permute-done
  383.8 8.6 copy.78
  400.5 8.0 collective-permute-start.3
  408.6 38.2 %collective-permute-done.3 = bf16[256,768]{1,0:T(8,128)(2,1)S(1)} collective-permute-done((bf16[256,768]{1,0:T(8,128)(2,1)S(1)}, bf16[256,768]{1,0:T(8,128)(2,1)S(1)}, u32[]{:S(2)}, u32[]{:S(2)}) %collective-permute-start.3) | collective-permute-done | bytes 393248 | tf_op jit(solution)/shard_map/ppermute | solution.py:204
  446.8 9.2 collective-permute-start.7
  455.9 9.5 collective-permute-done.4
  466.6 15.4 %collective-permute-start.8 = (bf16[256,768]{1,0:T(8,128)(2,1)S(1)}, bf16[256,768]{1,0:T(8,128)(2,1)}, u32[]{:S(2)}, u32[]{:S(2)}) collective-permute-start(bf16[256,768]{1,0:T(8,128)(2,1)S(1)} %collective-permute-done.7), channel_id=1, source_target_pairs={{1,0},{2,1},{3,2},{4,3},{5,4},{6,5},{7,6},{0,7},{9,8},{10,9},{11,1... | collective-permute-start | bytes 1179656 | tf_op jit(solution)/shard_map/ppermute | solution.py:206
  489.7 7.7 collective-permute-start.9
  540.6 60.3 %reduce-scatter.10.cloned.1.call-done = bf16[256,768]{1,0:T(8,128)(2,1)} async-done(((bf16[2048,768]{1,0:T(8,128)(2,1)}), bf16[256,768]{1,0:T(8,128)(2,1)}) %reduce-scatter.10.cloned.1.call-update) | async-done | bytes 393232 | tf_op jit(solution)/shard_map/reduce_scatter | solution.py:225
  602.3 75.6 %reduce-scatter.8.cloned.1.call-done = bf16[256,768]{1,0:T(8,128)(2,1)} async-done(((bf16[2048,768]{1,0:T(8,128)(2,1)}), bf16[256,768]{1,0:T(8,128)(2,1)}) %reduce-scatter.8.cloned.1.call-update) | async-done | bytes 393232 | tf_op jit(solution)/shard_map/reduce_scatter | solution.py:213
  685.9 6.2 broadcast_in_dim.196
  692.0 8.1 while.89
  706.4 249.3 %while.85 = (s32[]{:T(128)}, f32[256,1536]{1,0:T(8,128)}, f32[2048,1536]{0,1:T(8,128)}, s32[]{:T(128)}, s32[]{:T(128)}, /*index=5*/s32[]{:T(128)}, s32[]{:T(128)}, s32[]{:T(128)}, s32[]{:T(128)}) while((s32[]{:T(128)}, f32[256,1536]{1,0:T(8,128)}, f32[2048,1536]{0,1:T(8,128)}, s32[]{:T(128)}, s32[]{:T(128)}, /*index=5*/s32[]{:T(128)}, ...), condition=%wide.region_22.23_spmd, body=%wide.region_21.22_spmd.sunk | while | flops 1179656 | bytes 15728847 | solution.py:291
  712.1 28.8 %collective-permute-done.1 = bf16[256,1536]{1,0:T(8,128)(2,1)} collective-permute-done((bf16[256,1536]{1,0:T(8,128)(2,1)}, bf16[256,1536]{1,0:T(8,128)(2,1)}, u32[]{:S(2)}, u32[]{:S(2)}) %collective-permute-start.1) | collective-permute-done | bytes 786464 | tf_op jit(solution)/shard_map/while/body/eval_jaxpr/ppermute | solution.py:19
  749.1 27.5 %collective-permute-done.1 = bf16[256,1536]{1,0:T(8,128)(2,1)} collective-permute-done((bf16[256,1536]{1,0:T(8,128)(2,1)}, bf16[256,1536]{1,0:T(8,128)(2,1)}, u32[]{:S(2)}, u32[]{:S(2)}) %collective-permute-start.1) | collective-permute-done | bytes 786464 | tf_op jit(solution)/shard_map/while/body/eval_jaxpr/ppermute | solution.py:19
  784.8 28.7 %collective-permute-done.1 = bf16[256,1536]{1,0:T(8,128)(2,1)} collective-permute-done((bf16[256,1536]{1,0:T(8,128)(2,1)}, bf16[256,1536]{1,0:T(8,128)(2,1)}, u32[]{:S(2)}, u32[]{:S(2)}) %collective-permute-start.1) | collective-permute-done | bytes 786464 | tf_op jit(solution)/shard_map/while/body/eval_jaxpr/ppermute | solution.py:19
  821.7 29.9 %collective-permute-done.1 = bf16[256,1536]{1,0:T(8,128)(2,1)} collective-permute-done((bf16[256,1536]{1,0:T(8,128)(2,1)}, bf16[256,1536]{1,0:T(8,128)(2,1)}, u32[]{:S(2)}, u32[]{:S(2)}) %collective-permute-start.1) | collective-permute-done | bytes 786464 | tf_op jit(solution)/shard_map/while/body/eval_jaxpr/ppermute | solution.py:19
  859.8 28.3 %collective-permute-done.1 = bf16[256,1536]{1,0:T(8,128)(2,1)} collective-permute-done((bf16[256,1536]{1,0:T(8,128)(2,1)}, bf16[256,1536]{1,0:T(8,128)(2,1)}, u32[]{:S(2)}, u32[]{:S(2)}) %collective-permute-start.1) | collective-permute-done | bytes 786464 | tf_op jit(solution)/shard_map/while/body/eval_jaxpr/ppermute | solution.py:19
  896.2 26.3 %collective-permute-done.1 = bf16[256,1536]{1,0:T(8,128)(2,1)} collective-permute-done((bf16[256,1536]{1,0:T(8,128)(2,1)}, bf16[256,1536]{1,0:T(8,128)(2,1)}, u32[]{:S(2)}, u32[]{:S(2)}) %collective-permute-start.1) | collective-permute-done | bytes 786464 | tf_op jit(solution)/shard_map/while/body/eval_jaxpr/ppermute | solution.py:19
  930.7 22.4 %collective-permute-done.1 = bf16[256,1536]{1,0:T(8,128)(2,1)} collective-permute-done((bf16[256,1536]{1,0:T(8,128)(2,1)}, bf16[256,1536]{1,0:T(8,128)(2,1)}, u32[]{:S(2)}, u32[]{:S(2)}) %collective-permute-start.1) | collective-permute-done | bytes 786464 | tf_op jit(solution)/shard_map/while/body/eval_jaxpr/ppermute | solution.py:19
  979.9 46.1 %all-reduce.4 = (f32[768,3,3]{0,2,1:T(4,128)S(1)}, f32[768,2]{0,1:T(2,128)S(1)}, f32[768,2]{0,1:T(2,128)S(1)}) all-reduce(f32[768,3,3]{0,2,1:T(4,128)S(1)} %maximum_bitcast_fusion, f32[768,2]{0,1:T(2,128)S(1)} %pad_maximum_fusion.3, f32[768,2]{0,1:T(2,128)S(1)} %pad_maximum_fusion.4), channel_id=6, replica_groups=mesh['dp'=4,'mp'=8] {'dp','mp'}, use_global_device_ids=true, to_apply=%region_30.31.clone | all-reduce | flops 9984 | bytes 79872
  1030.2 67.4 %reduce-scatter.12.cloned.1.call-done = f32[24,2304]{1,0:T(8,128)} async-done(((f32[768,2304]{1,0:T(8,128)}), f32[24,2304]{1,0:T(8,128)}) %reduce-scatter.12.cloned.1.call-update) | async-done | bytes 221200 | tf_op jit(solution)/shard_map/reduce_scatter | solution.py:306
  (265 shorter events, 242.5 us)
Async XLA Ops:
  7.2 504.1 %copy-start = (bf16[768,384]{1,0:T(8,128)(2,1)S(1)}, bf16[768,384]{1,0:T(8,128)(2,1)}, u32[]{:S(2)}) copy-start(bf16[768,384]{1,0:T(8,128)(2,1)} %param.29) | copy-start | bytes 1769476
  7.2 215.3 %all-gather.6.cloned.1.call-start = ((), (), s32[]{:S(2)}) async-start(), calls=%async_computation.4 | async-start | bytes 3649536 | tf_op jit(solution)/shard_map/all_gather | solution.py:104
  7.9 390.2 %all-gather.8.cloned.1.call-start = ((), (), s32[]{:S(2)}) async-start(), calls=%async_computation.5 | async-start | bytes 1216512 | tf_op jit(solution)/shard_map/all_gather | solution.py:105
  8.7 508.0 %all-gather.10.cloned.1.call-start = ((), (), s32[]{:S(2)}) async-start(), calls=%async_computation.7 | async-start | bytes 3538944 | tf_op jit(solution)/shard_map/all_gather | solution.py:220
  9.4 591.5 %reduce-scatter.10.cloned.1.call-start = ((), (), s32[]{:S(2)}) async-start(), calls=%async_computation.8 | async-start | bytes 3538944 | tf_op jit(solution)/shard_map/reduce_scatter | solution.py:225
  227.2 4.9 collective-permute-start.2
  240.0 18.4 %collective-permute-start = (bf16[256,1536]{1,0:T(8,128)(2,1)S(1)}, bf16[256,1536]{1,0:T(8,128)(2,1)S(1)}, u32[]{:S(2)}, u32[]{:S(2)}) collective-permute-start(bf16[256,1536]{1,0:T(8,128)(2,1)S(1)} %get-tuple-element.1378), channel_id=1, source_target_pairs={{0,1},{1,2},{2,3},{3,4},{4,5},{5,6},{6,7},{8,9},{9,10},{10,11},{11... | collective-permute-start | bytes 2359304 | tf_op jit(solution)/shard_map/while/body/eval_jaxpr/ppermute | solution.py:19
  259.4 19.7 %collective-permute-start = (bf16[256,1536]{1,0:T(8,128)(2,1)S(1)}, bf16[256,1536]{1,0:T(8,128)(2,1)S(1)}, u32[]{:S(2)}, u32[]{:S(2)}) collective-permute-start(bf16[256,1536]{1,0:T(8,128)(2,1)S(1)} %get-tuple-element.1378), channel_id=1, source_target_pairs={{0,1},{1,2},{2,3},{3,4},{4,5},{5,6},{6,7},{8,9},{9,10},{10,11},{11... | collective-permute-start | bytes 2359304 | tf_op jit(solution)/shard_map/while/body/eval_jaxpr/ppermute | solution.py:19
  280.1 20.8 %collective-permute-start = (bf16[256,1536]{1,0:T(8,128)(2,1)S(1)}, bf16[256,1536]{1,0:T(8,128)(2,1)S(1)}, u32[]{:S(2)}, u32[]{:S(2)}) collective-permute-start(bf16[256,1536]{1,0:T(8,128)(2,1)S(1)} %get-tuple-element.1378), channel_id=1, source_target_pairs={{0,1},{1,2},{2,3},{3,4},{4,5},{5,6},{6,7},{8,9},{9,10},{10,11},{11... | collective-permute-start | bytes 2359304 | tf_op jit(solution)/shard_map/while/body/eval_jaxpr/ppermute | solution.py:19
  301.8 22.0 %collective-permute-start = (bf16[256,1536]{1,0:T(8,128)(2,1)S(1)}, bf16[256,1536]{1,0:T(8,128)(2,1)S(1)}, u32[]{:S(2)}, u32[]{:S(2)}) collective-permute-start(bf16[256,1536]{1,0:T(8,128)(2,1)S(1)} %get-tuple-element.1378), channel_id=1, source_target_pairs={{0,1},{1,2},{2,3},{3,4},{4,5},{5,6},{6,7},{8,9},{9,10},{10,11},{11... | collective-permute-start | bytes 2359304 | tf_op jit(solution)/shard_map/while/body/eval_jaxpr/ppermute | solution.py:19
  324.8 21.5 %collective-permute-start = (bf16[256,1536]{1,0:T(8,128)(2,1)S(1)}, bf16[256,1536]{1,0:T(8,128)(2,1)S(1)}, u32[]{:S(2)}, u32[]{:S(2)}) collective-permute-start(bf16[256,1536]{1,0:T(8,128)(2,1)S(1)} %get-tuple-element.1378), channel_id=1, source_target_pairs={{0,1},{1,2},{2,3},{3,4},{4,5},{5,6},{6,7},{8,9},{9,10},{10,11},{11... | collective-permute-start | bytes 2359304 | tf_op jit(solution)/shard_map/while/body/eval_jaxpr/ppermute | solution.py:19
  347.3 20.6 %collective-permute-start = (bf16[256,1536]{1,0:T(8,128)(2,1)S(1)}, bf16[256,1536]{1,0:T(8,128)(2,1)S(1)}, u32[]{:S(2)}, u32[]{:S(2)}) collective-permute-start(bf16[256,1536]{1,0:T(8,128)(2,1)S(1)} %get-tuple-element.1378), channel_id=1, source_target_pairs={{0,1},{1,2},{2,3},{3,4},{4,5},{5,6},{6,7},{8,9},{9,10},{10,11},{11... | collective-permute-start | bytes 2359304 | tf_op jit(solution)/shard_map/while/body/eval_jaxpr/ppermute | solution.py:19
  369.0 13.9 %collective-permute-start = (bf16[256,1536]{1,0:T(8,128)(2,1)S(1)}, bf16[256,1536]{1,0:T(8,128)(2,1)S(1)}, u32[]{:S(2)}, u32[]{:S(2)}) collective-permute-start(bf16[256,1536]{1,0:T(8,128)(2,1)S(1)} %get-tuple-element.1378), channel_id=1, source_target_pairs={{0,1},{1,2},{2,3},{3,4},{4,5},{5,6},{6,7},{8,9},{9,10},{10,11},{11... | collective-permute-start | bytes 2359304 | tf_op jit(solution)/shard_map/while/body/eval_jaxpr/ppermute | solution.py:19
  400.5 46.2 %collective-permute-start.3 = (bf16[256,768]{1,0:T(8,128)(2,1)S(1)}, bf16[256,768]{1,0:T(8,128)(2,1)S(1)}, u32[]{:S(2)}, u32[]{:S(2)}) collective-permute-start(bf16[256,768]{1,0:T(8,128)(2,1)S(1)} %add_convert_fusion.2), channel_id=1, source_target_pairs={{0,1},{1,2},{2,3},{3,4},{4,5},{5,6},{6,7},{7,0},{8,9},{9,10},{10,1... | collective-permute-start | bytes 1179656 | tf_op jit(solution)/shard_map/ppermute | solution.py:204
  446.8 18.7 %collective-permute-start.4 = (bf16[256,768]{1,0:T(8,128)(2,1)S(1)}, bf16[256,768]{1,0:T(8,128)(2,1)S(1)}, u32[]{:S(2)}, u32[]{:S(2)}) collective-permute-start(bf16[256,768]{1,0:T(8,128)(2,1)S(1)} %collective-permute-done.3), channel_id=1, source_target_pairs={{0,1},{1,2},{2,3},{3,4},{4,5},{5,6},{6,7},{7,0},{8,9},{9,10},{10,1... | collective-permute-start | bytes 1179656 | tf_op jit(solution)/shard_map/ppermute | solution.py:204
  446.8 19.8 %collective-permute-start.7 = (bf16[256,768]{1,0:T(8,128)(2,1)S(1)}, bf16[256,768]{1,0:T(8,128)(2,1)S(1)}, u32[]{:S(2)}, u32[]{:S(2)}) collective-permute-start(bf16[256,768]{1,0:T(8,128)(2,1)S(1)} %add_convert_fusion.2), channel_id=1, source_target_pairs={{1,0},{2,1},{3,2},{4,3},{5,4},{6,5},{7,6},{0,7},{9,8},{10,9},{11,1... | collective-permute-start | bytes 1179656 | tf_op jit(solution)/shard_map/ppermute | solution.py:206
  465.4 17.8 %collective-permute-start.5 = (bf16[256,768]{1,0:T(8,128)(2,1)S(1)}, bf16[256,768]{1,0:T(8,128)(2,1)}, u32[]{:S(2)}, u32[]{:S(2)}) collective-permute-start(bf16[256,768]{1,0:T(8,128)(2,1)S(1)} %collective-permute-done.4), channel_id=1, source_target_pairs={{0,1},{1,2},{2,3},{3,4},{4,5},{5,6},{6,7},{7,0},{8,9},{9,10},{10,1... | collective-permute-start | bytes 1179656 | tf_op jit(solution)/shard_map/ppermute | solution.py:204
  466.6 23.1 %collective-permute-start.8 = (bf16[256,768]{1,0:T(8,128)(2,1)S(1)}, bf16[256,768]{1,0:T(8,128)(2,1)}, u32[]{:S(2)}, u32[]{:S(2)}) collective-permute-start(bf16[256,768]{1,0:T(8,128)(2,1)S(1)} %collective-permute-done.7), channel_id=1, source_target_pairs={{1,0},{2,1},{3,2},{4,3},{5,4},{6,5},{7,6},{0,7},{9,8},{10,9},{11,1... | collective-permute-start | bytes 1179656 | tf_op jit(solution)/shard_map/ppermute | solution.py:206
  483.2 14.3 %collective-permute-start.6 = (bf16[256,768]{1,0:T(8,128)(2,1)}, bf16[256,768]{1,0:T(8,128)(2,1)}, u32[]{:S(2)}, u32[]{:S(2)}) collective-permute-start(bf16[256,768]{1,0:T(8,128)(2,1)} %collective-permute-done.5), channel_id=1, source_target_pairs={{0,1},{1,2},{2,3},{3,4},{4,5},{5,6},{6,7},{7,0},{8,9},{9,10},{10,1... | collective-permute-start | bytes 1179656 | tf_op jit(solution)/shard_map/ppermute | solution.py:204
  489.7 16.5 %collective-permute-start.9 = (bf16[256,768]{1,0:T(8,128)(2,1)}, bf16[256,768]{1,0:T(8,128)(2,1)S(1)}, u32[]{:S(2)}, u32[]{:S(2)}) collective-permute-start(bf16[256,768]{1,0:T(8,128)(2,1)} %collective-permute-done.8), channel_id=1, source_target_pairs={{1,0},{2,1},{3,2},{4,3},{5,4},{6,5},{7,6},{0,7},{9,8},{10,9},{11,1... | collective-permute-start | bytes 1179656 | tf_op jit(solution)/shard_map/ppermute | solution.py:206
  525.0 152.9 %reduce-scatter.8.cloned.1.call-start = ((), (), s32[]{:S(2)}) async-start(), calls=%async_computation.6 | async-start | bytes 3538944 | tf_op jit(solution)/shard_map/reduce_scatter | solution.py:213
  531.4 441.7 %all-reduce.8.cloned.1.call-start = ((), (), s32[]{:S(2)}) async-start(), calls=%async_computation.11 | async-start | bytes 2359296 | tf_op jit(solution)/shard_map/psum | solution.py:229
  540.6 489.7 %reduce-scatter.14.cloned.1.call-start = ((), (), s32[]{:S(2)}) async-start(), calls=%async_computation.10 | async-start | bytes 2433024 | tf_op jit(solution)/shard_map/reduce_scatter | solution.py:307
  706.3 391.3 %reduce-scatter.12.cloned.1.call-start = ((), (), s32[]{:S(2)}) async-start(), calls=%async_computation.9 | async-start | bytes 7299072 | tf_op jit(solution)/shard_map/reduce_scatter | solution.py:306
  708.8 32.1 %collective-permute-start.1 = (bf16[256,1536]{1,0:T(8,128)(2,1)}, bf16[256,1536]{1,0:T(8,128)(2,1)}, u32[]{:S(2)}, u32[]{:S(2)}) collective-permute-start(bf16[256,1536]{1,0:T(8,128)(2,1)} %convert_element_type.232), channel_id=1, source_target_pairs={{1,0},{2,1},{3,2},{4,3},{5,4},{6,5},{7,6},{9,8},{10,9},{11,10},{12... | collective-permute-start | bytes 2359304 | tf_op jit(solution)/shard_map/while/body/eval_jaxpr/ppermute | solution.py:19
  745.8 30.7 %collective-permute-start.1 = (bf16[256,1536]{1,0:T(8,128)(2,1)}, bf16[256,1536]{1,0:T(8,128)(2,1)}, u32[]{:S(2)}, u32[]{:S(2)}) collective-permute-start(bf16[256,1536]{1,0:T(8,128)(2,1)} %convert_element_type.232), channel_id=1, source_target_pairs={{1,0},{2,1},{3,2},{4,3},{5,4},{6,5},{7,6},{9,8},{10,9},{11,10},{12... | collective-permute-start | bytes 2359304 | tf_op jit(solution)/shard_map/while/body/eval_jaxpr/ppermute | solution.py:19
  781.5 32.0 %collective-permute-start.1 = (bf16[256,1536]{1,0:T(8,128)(2,1)}, bf16[256,1536]{1,0:T(8,128)(2,1)}, u32[]{:S(2)}, u32[]{:S(2)}) collective-permute-start(bf16[256,1536]{1,0:T(8,128)(2,1)} %convert_element_type.232), channel_id=1, source_target_pairs={{1,0},{2,1},{3,2},{4,3},{5,4},{6,5},{7,6},{9,8},{10,9},{11,10},{12... | collective-permute-start | bytes 2359304 | tf_op jit(solution)/shard_map/while/body/eval_jaxpr/ppermute | solution.py:19
  818.4 33.2 %collective-permute-start.1 = (bf16[256,1536]{1,0:T(8,128)(2,1)}, bf16[256,1536]{1,0:T(8,128)(2,1)}, u32[]{:S(2)}, u32[]{:S(2)}) collective-permute-start(bf16[256,1536]{1,0:T(8,128)(2,1)} %convert_element_type.232), channel_id=1, source_target_pairs={{1,0},{2,1},{3,2},{4,3},{5,4},{6,5},{7,6},{9,8},{10,9},{11,10},{12... | collective-permute-start | bytes 2359304 | tf_op jit(solution)/shard_map/while/body/eval_jaxpr/ppermute | solution.py:19
  856.5 31.5 %collective-permute-start.1 = (bf16[256,1536]{1,0:T(8,128)(2,1)}, bf16[256,1536]{1,0:T(8,128)(2,1)}, u32[]{:S(2)}, u32[]{:S(2)}) collective-permute-start(bf16[256,1536]{1,0:T(8,128)(2,1)} %convert_element_type.232), channel_id=1, source_target_pairs={{1,0},{2,1},{3,2},{4,3},{5,4},{6,5},{7,6},{9,8},{10,9},{11,10},{12... | collective-permute-start | bytes 2359304 | tf_op jit(solution)/shard_map/while/body/eval_jaxpr/ppermute | solution.py:19
  892.9 29.6 %collective-permute-start.1 = (bf16[256,1536]{1,0:T(8,128)(2,1)}, bf16[256,1536]{1,0:T(8,128)(2,1)}, u32[]{:S(2)}, u32[]{:S(2)}) collective-permute-start(bf16[256,1536]{1,0:T(8,128)(2,1)} %convert_element_type.232), channel_id=1, source_target_pairs={{1,0},{2,1},{3,2},{4,3},{5,4},{6,5},{7,6},{9,8},{10,9},{11,10},{12... | collective-permute-start | bytes 2359304 | tf_op jit(solution)/shard_map/while/body/eval_jaxpr/ppermute | solution.py:19
  927.4 25.7 %collective-permute-start.1 = (bf16[256,1536]{1,0:T(8,128)(2,1)}, bf16[256,1536]{1,0:T(8,128)(2,1)}, u32[]{:S(2)}, u32[]{:S(2)}) collective-permute-start(bf16[256,1536]{1,0:T(8,128)(2,1)} %convert_element_type.232), channel_id=1, source_target_pairs={{1,0},{2,1},{3,2},{4,3},{5,4},{6,5},{7,6},{9,8},{10,9},{11,10},{12... | collective-permute-start | bytes 2359304 | tf_op jit(solution)/shard_map/while/body/eval_jaxpr/ppermute | solution.py:19
  956.7 6.4 collective-permute-start.10
  (24 other events, 1761.8 us)
Sparse Core Ops, SparseCore 0:
  11.0 63.0 all-gather.5
  77.0 52.9 all-gather.7
  132.2 66.4 all-gather.9
  525.1 75.7 reduce-scatter.9
  604.3 73.5 reduce-scatter.7
  680.1 36.6 all-reduce.7
  722.7 165.0 reduce-scatter.13
  973.3 124.3 reduce-scatter.11
